TPU v7x, 128 devices: a whole 4x4x4 slice. The times are simulated.
128 devices in a mesh: section: 2 (over core), dp: 16 (over y, x), mp: 4 (over z).
Axes of the slice: x: 4, y: 4, z: 4, core: 2. Of those that a mesh axis runs over, the one named last changes fastest.
Arguments:
- patches: bfloat16 [8192, 1280], P(('section', 'dp', 'mp')), may hold values from -6 to 6
- image_units: int32 [128, 3], P(('section', 'dp', 'mp')), may hold values from 1 to 8, 16 in all within a row
- v_gain: float32 [1280], replicated, may hold values from 0.5 to 1.5
- v_qkv: bfloat16 [1280, 3840], replicated, may hold values from -0.15625 to 0.15625
- v_out: bfloat16 [1280, 1280], replicated, may hold values from -0.15625 to 0.15625
- merge_gain: float32 [1280], replicated, may hold values from 0.5 to 1.5
- w_merge: bfloat16 [5120, 8192], P('dp', 'mp'), may hold values from -0.078125 to 0.078125
- routes: int32 [2048, 1], P(('section', 'dp', 'mp')), may hold values from 0 to 15; in each aligned block of 1024 rows (0 to 1023, 1024 to 2047, ...) at most 128 rows name the same one
- text: bfloat16 [4096, 8192], P(('section', 'dp'), 'mp'), may hold values from -6 to 6
- seq_lengths: int32 [32, 3], P(('section', 'dp')), may hold values from 1 to 64, 128 in all within a row
- lang_gain: float32 [2, 8192], P('section'), may hold values from 0.5 to 1.5
- w_qkv: bfloat16 [2, 8192, 5120], P('section', 'dp', 'mp'), may hold values from -0.0625 to 0.0625
- wo_t: bfloat16 [2, 8192, 4096], P('section', 'dp', 'mp'), may hold values from -0.09375 to 0.09375
- row_grads: bfloat16 [4096, 8192], P(('section', 'dp'), 'mp'), may hold values from -6 to 6
Outputs:
- final_hidden: bfloat16 [4096, 8192], P(('section', 'dp'), 'mp')
- merged_grads: bfloat16 [2048, 8192], P(('section', 'dp', 'mp'))
Inputs may be any that keep to these rules, and one draw needn't show every extreme that they name: `image_units`: each row sums to 16. `routes`: among the 1024 rows of one section index (aligned blocks), at most 128 name one group; in some section index one group is named by exactly 128. `seq_lengths`: each row sums to 128.
All inputs are finite; a program needn't handle non-finite values.
Results may differ from a plain program's by a relative error of at most 0.03.
Values may be sent and summed in bfloat16 or wider, within the bound.
A program may use at most 192 MiB of HBM per device.

v0:
```python
import math
import jax
import jax.numpy as jnp
from jax import lax
from jax.sharding import PartitionSpec as P

QH = 32
KVH = 4
HD = 128
VD = 1280
VH = 16
VHD = 80
MERGE = 4
EPSILON = 1e-06


def passed_along(value, axis, steps):
    count = lax.axis_size(axis)
    initial, last = (max(0, -steps), min(count, count - steps))
    return lax.ppermute(value, axis, [(source, source + steps) for source in range(initial, last)])


def broadcast(block, axis, owner):
    block = jnp.where(lax.axis_index(axis) == owner, block, jnp.zeros_like(block))
    return lax.psum(block, axis)


def layer_norm(values, norm_gain):
    values = values.astype(jnp.float32)
    centre = jnp.mean(values, axis=-1, keepdims=True)
    centred = values - centre
    variance = jnp.mean(centred * centred, axis=-1, keepdims=True)
    return centred * lax.rsqrt(variance + EPSILON) * norm_gain


def rms_norm(values, norm_gain):
    values = values.astype(jnp.float32)
    return (
        values * lax.rsqrt(jnp.mean(values * values, axis=-1, keepdims=True) + EPSILON) * norm_gain
    )


def segment_of(lengths, amount):
    boundary = jnp.cumsum(lengths.astype(jnp.int32))
    positions = jnp.arange(amount, dtype=jnp.int32)
    return jnp.sum((positions[:, None] >= boundary[None, :]).astype(jnp.int32), axis=1)


def vision_rows(patches, units, v_gain, v_qkv, v_out, merge_gain):
    amount = patches.shape[0]
    merged_count = amount // MERGE
    unit_image = segment_of(units, merged_count)
    image_ids = jnp.broadcast_to(unit_image[:, None], (merged_count, MERGE)).reshape(amount)
    v_normed = layer_norm(patches, v_gain).astype(jnp.bfloat16)
    projected = jnp.dot(v_normed, v_qkv, preferred_element_type=jnp.float32).astype(jnp.bfloat16)
    projected = projected.reshape(amount, 3, VH, VHD)
    scores = jnp.einsum(
        "qhd,khd->hqk", projected[:, 0], projected[:, 1], preferred_element_type=jnp.float32
    ) / math.sqrt(VHD)
    allowed = image_ids[:, None] == image_ids[None, :]
    scores = jnp.where(allowed[None], scores, -1e30)
    weights = jax.nn.softmax(scores, axis=-1).astype(jnp.bfloat16)
    attended = (
        jnp.einsum("hqk,khd->qhd", weights, projected[:, 2], preferred_element_type=jnp.float32)
        .astype(jnp.bfloat16)
        .reshape(amount, VD)
    )
    update = jnp.dot(attended, v_out, preferred_element_type=jnp.float32)
    v_hidden = (patches.astype(jnp.float32) + update).astype(jnp.bfloat16)
    merged = layer_norm(v_hidden, merge_gain).astype(jnp.bfloat16)
    return merged.reshape(merged_count, MERGE * VD)


def attend(projected, lengths):
    seq_rows = projected.shape[0]
    group_size = QH // KVH
    kv_here = projected.shape[1] // ((group_size + 2) * HD)
    heads_view = projected.reshape(seq_rows, kv_here, group_size + 2, HD)
    scores = jnp.einsum(
        "tkgd,skd->kgts",
        heads_view[:, :, :group_size],
        heads_view[:, :, group_size],
        preferred_element_type=jnp.float32,
    ) * (1.0 / math.sqrt(HD))
    seq_ids = segment_of(lengths, seq_rows)
    positions = jnp.arange(seq_rows, dtype=jnp.int32)
    allowed = (seq_ids[:, None] == seq_ids[None, :]) & (positions[:, None] >= positions[None, :])
    scores = jnp.where(allowed[None, None], scores, -1e30)
    weights = jax.nn.softmax(scores, axis=-1).astype(jnp.bfloat16)
    attended = jnp.einsum(
        "kgts,skd->tkgd",
        weights,
        heads_view[:, :, group_size + 1],
        preferred_element_type=jnp.float32,
    ).astype(jnp.bfloat16)
    return attended.reshape(seq_rows, kv_here * group_size * HD)


def shards(
    patches,
    image_units,
    v_gain,
    v_qkv,
    v_out,
    merge_gain,
    w_merge,
    routes,
    text,
    seq_lengths,
    lang_gain,
    w_qkv,
    wo_t,
    row_grads,
):
    merged = vision_rows(patches, image_units[0], v_gain, v_qkv, v_out, merge_gain)
    all_rows, all_routes = (
        lax.all_gather(merged, ("dp", "mp"), axis=0, tiled=True),
        lax.all_gather(routes, ("dp", "mp"), axis=0, tiled=True),
    )
    target = all_routes[:, 0]
    section_rows = target.shape[0]
    row_order = jnp.arange(section_rows, dtype=jnp.int32)
    matching = target[:, None] == target[None, :]
    position = jnp.sum(
        (matching & (row_order[:, None] > row_order[None, :])).astype(jnp.int32), axis=1
    )
    seq_rows = text.shape[0]
    slot_index = target * seq_rows + position
    group_here = lax.axis_index("dp")
    dp_count = lax.axis_size("dp")
    slice_width = w_merge.shape[0]
    row_slice = lax.dynamic_slice_in_dim(all_rows, group_here * slice_width, slice_width, 1)
    wanted = jnp.arange(seq_rows * lax.axis_size("dp"), dtype=jnp.int32)
    picker = (slot_index[None, :] == wanted[:, None]).astype(jnp.bfloat16)
    picked = jnp.dot(picker, row_slice, preferred_element_type=jnp.float32).astype(jnp.bfloat16)
    image_rows = lax.psum_scatter(
        jnp.dot(picked, w_merge, preferred_element_type=jnp.float32).astype(jnp.bfloat16),
        "dp",
        scatter_dimension=0,
        tiled=True,
    )
    present = jnp.sum((target == group_here).astype(jnp.int32))
    positions = jnp.arange(seq_rows, dtype=jnp.int32)
    entry_rows = jnp.where((positions < present)[:, None], image_rows, text)
    gathered = (
        lax.all_gather(w_qkv, "dp", axis=1, tiled=True),
        lax.all_gather(wo_t, "dp", axis=1, tiled=True),
    )
    qkv_weight = gathered[0][0]
    out_weight = gathered[1][0]
    norm_gain = lang_gain[0]
    sections = lax.axis_size("section")
    section_here = lax.axis_index("section")
    is_first = section_here == 0
    lengths_here = seq_lengths[0]
    entry_all, lengths_all = (
        lax.all_gather(entry_rows, "section", axis=0, tiled=True),
        lax.all_gather(seq_lengths, "section", axis=0, tiled=True),
    )
    carried = jnp.zeros_like(entry_rows)
    carried_lengths = lengths_here
    finished = []
    for section_step in range(2 * sections - 1):
        if section_step > 0:
            carried, carried_lengths = passed_along((carried, carried_lengths), "section", 1)
        if section_step < sections:
            incoming = entry_all[section_step * seq_rows : (section_step + 1) * seq_rows]
            incoming_lengths = lengths_all[section_step]
            carried = jnp.where(is_first, incoming, carried)
            carried_lengths = jnp.where(is_first, incoming_lengths, carried_lengths)
        features = lax.all_gather(carried, "mp", axis=1, tiled=True)
        normed = rms_norm(features, norm_gain).astype(jnp.bfloat16)
        projected = jnp.dot(normed, qkv_weight, preferred_element_type=jnp.float32)
        attended = attend(projected.astype(jnp.bfloat16), carried_lengths)
        partial_value = lax.dot_general(
            attended, out_weight, (((1,), (1,)), ((), ())), preferred_element_type=jnp.float32
        )
        update = lax.psum_scatter(
            partial_value.astype(jnp.bfloat16), "mp", scatter_dimension=1, tiled=True
        ).astype(jnp.float32)
        carried = (carried.astype(jnp.float32) + update).astype(jnp.bfloat16)
        if section_step >= sections - 1:
            finished.append(carried)
    returned_rows = broadcast(jnp.stack(finished), "section", sections - 1)
    final_hidden = lax.dynamic_index_in_dim(returned_rows, section_here, 0, keepdims=False)
    columns = row_grads.shape[1]
    picker = ((target == group_here)[:, None] & (position[:, None] == positions[None, :])).astype(
        jnp.bfloat16
    )
    outgoing = jnp.dot(picker, row_grads, preferred_element_type=jnp.float32).astype(jnp.bfloat16)
    outgoing = outgoing.reshape(dp_count, section_rows // dp_count, columns)
    returned = lax.all_to_all(
        lax.all_to_all(outgoing, "dp", split_axis=0, concat_axis=0, tiled=True),
        "mp",
        split_axis=1,
        concat_axis=2,
        tiled=True,
    )
    merged_grads = jnp.sum(returned.astype(jnp.float32), axis=0).astype(jnp.bfloat16)
    return (final_hidden, merged_grads)


def solution(mesh):
    in_specs = (
        P(("section", "dp", "mp"), None),
        P(("section", "dp", "mp"), None),
        P(),
        P(),
        P(),
        P(),
        P("dp", "mp"),
        P(("section", "dp", "mp"), None),
        P(("section", "dp"), "mp"),
        P(("section", "dp"), None),
        P("section", None),
        P("section", "dp", "mp"),
        P("section", "dp", "mp"),
        P(("section", "dp"), "mp"),
    )
    out_specs = (P(("section", "dp"), "mp"), P(("section", "dp", "mp"), None))
    return jax.shard_map(shards, mesh=mesh, in_specs=in_specs, out_specs=out_specs, check_vma=False)
```

profile of v0, /device:TPU:0, one launch (start us, length us, event | category | flops | bytes accessed | tf_op | source)
XLA Modules:
  0.0 799.6 jit_solution(8067572202809848577)
XLA Ops:
  9.6 6.6 convolution_convert_fusion.1
  34.4 24.9 %all-reduce = s32[1024]{0:T(1024)S(1)} all-reduce(s32[1024]{0:T(1024)S(1)} %bitcast_dynamic-update-slice_fusion), channel_id=1, replica_groups=mesh['section'=2,'dp'=16,'mp'=4] {'dp','mp'}, use_global_device_ids=true, to_apply=%add | all-reduce | flops 1024 | bytes 8192 | tf_op jit(solution)/shard_map/squeeze | solution.py:120
  60.4 60.5 %all-gather.9.cloned.1.call-done = bf16[1024,5120]{1,0:T(8,128)(2,1)} async-done(((bf16[16,5120]{1,0:T(8,128)(2,1)}), bf16[1024,5120]{1,0:T(8,128)(2,1)}) %all-gather.9.cloned.1.call-update) | async-done | bytes 10485776 | tf_op jit(solution)/shard_map/all_gather | solution.py:117
  120.9 10.7 %convolution_convert_fusion = bf16[2048,2048]{1,0:T(8,128)(2,1)} fusion(bf16[320,2048]{1,0:T(8,128)(2,1)} %param.20, s32[1024]{0:T(1024)S(1)} %get-tuple-element.7, bf16[1024,5120]{1,0:T(8,128)(2,1)} %all-gather.9.cloned.1.call-done, s32[]{:T(128)S(6)} %select_n.69), kind=kOutput, calls=%fused_computation.18 | convolution fusion | flops 4033478656 | bytes 10489860 | tf_op jit(solution)/shard_map/dot_general | solution.py:137
  132.4 83.8 %reduce-scatter.5.cloned.1.call-done = bf16[128,2048]{1,0:T(8,128)(2,1)} async-done(((bf16[2048,2048]{1,0:T(8,128)(2,1)}), bf16[128,2048]{1,0:T(8,128)(2,1)}) %reduce-scatter.5.cloned.1.call-update) | async-done | bytes 524304 | tf_op jit(solution)/shard_map/reduce_scatter | solution.py:136
  218.3 11.4 %all-gather.11.cloned.1.call-done = bf16[256,2048]{1,0:T(8,128)(2,1)} async-done(((bf16[128,2048]{1,0:T(8,128)(2,1)}), bf16[256,2048]{1,0:T(8,128)(2,1)}) %all-gather.11.cloned.1.call-update) | async-done | bytes 1048592 | tf_op jit(solution)/shard_map/all_gather | solution.py:157
  235.4 28.8 %all-gather.13.cloned.1.call-done = bf16[128,8192]{1,0:T(8,128)(2,1)} async-done(((bf16[128,2048]{1,0:T(8,128)(2,1)}), bf16[128,8192]{1,0:T(8,128)(2,1)}) %all-gather.13.cloned.1.call-update) | async-done | bytes 2097168 | tf_op jit(solution)/shard_map/all_gather | solution.py:171
  266.3 132.4 %all-gather.15.cloned.1.call-done = bf16[1,8192,1280]{2,1,0:T(8,128)(2,1)} async-done(((bf16[1,512,1280]{2,1,0:T(8,128)(2,1)}), bf16[1,8192,1280]{2,1,0:T(8,128)(2,1)}) %all-gather.15.cloned.1.call-update) | async-done | bytes 20971536 | tf_op jit(solution)/shard_map/all_gather | solution.py:146
  398.7 10.6 %fusion.35 = bf16[128,1280]{1,0:T(8,128)(2,1)S(1)} fusion(bf16[1,8192,1280]{2,1,0:T(8,128)(2,1)} %all-gather.15.cloned.1.call-done, bf16[128,8192]{1,0:T(8,128)(2,1)} %all-gather.13.cloned.1.call-done, f32[8192]{0:T(1024)S(1)} %bitcast.203, f32[128]{0:T(128)S(1)} %add_rsqrt_fusion.2), kind=kOutput, calls=%fused_computation.41 | convolution fusion | flops 2688712704 | bytes 23429632 | tf_op jit(solution)/shard_map/dot_general | solution.py:173
  410.1 101.6 %all-gather.17.cloned.1.call-done = bf16[1,8192,1024]{2,1,0:T(8,128)(2,1)} async-done(((bf16[1,512,1024]{2,1,0:T(8,128)(2,1)}), bf16[1,8192,1024]{2,1,0:T(8,128)(2,1)}) %all-gather.17.cloned.1.call-update) | async-done | bytes 16777232 | tf_op jit(solution)/shard_map/all_gather | solution.py:147
  511.7 12.8 %fusion.13 = bf16[128,8192]{1,0:T(8,128)(2,1)} fusion(bf16[128,1024]{0,1:T(8,128)(2,1)S(1)} %bitcast.197, bf16[1,8192,1024]{2,1,0:T(8,128)(2,1)} %all-gather.17.cloned.1.call-done), kind=kOutput, calls=%fused_computation.13 | convolution fusion | flops 2148532224 | bytes 19136512 | tf_op jit(solution)/shard_map/dot_general | solution.py:175
  524.6 29.7 %reduce-scatter.7.cloned.1.call-done = bf16[128,2048]{1,0:T(8,128)(2,1)} async-done(((bf16[128,8192]{1,0:T(8,128)(2,1)}), bf16[128,2048]{1,0:T(8,128)(2,1)}) %reduce-scatter.7.cloned.1.call-update) | async-done | bytes 524304 | tf_op jit(solution)/shard_map/reduce_scatter | solution.py:178
  563.2 27.3 %all-gather.19.cloned.1.call-done = bf16[128,8192]{1,0:T(8,128)(2,1)} async-done(((bf16[128,2048]{1,0:T(8,128)(2,1)}), bf16[128,8192]{1,0:T(8,128)(2,1)}) %all-gather.19.cloned.1.call-update) | async-done | bytes 2097168 | tf_op jit(solution)/shard_map/all_gather | solution.py:171
  592.6 10.6 %fusion.38 = bf16[128,1280]{1,0:T(8,128)(2,1)S(1)} fusion(bf16[1,8192,1280]{2,1,0:T(8,128)(2,1)} %all-gather.15.cloned.1.call-done, bf16[128,8192]{1,0:T(8,128)(2,1)} %all-gather.19.cloned.1.call-done, f32[128]{0:T(128)S(1)} %add_rsqrt_fusion.1, f32[8192]{0:T(1024)S(1)} %bitcast.204), kind=kOutput, calls=%fused_computation.42 | convolution fusion | flops 2688712704 | bytes 23429632 | tf_op jit(solution)/shard_map/dot_general | solution.py:173
  604.0 12.8 %fusion.16 = bf16[128,8192]{1,0:T(8,128)(2,1)} fusion(bf16[128,1024]{0,1:T(8,128)(2,1)S(1)} %bitcast.199, bf16[1,8192,1024]{2,1,0:T(8,128)(2,1)} %all-gather.17.cloned.1.call-done), kind=kOutput, calls=%fused_computation.14 | convolution fusion | flops 2148532224 | bytes 19136512 | tf_op jit(solution)/shard_map/dot_general | solution.py:175
  616.9 29.9 %reduce-scatter.9.cloned.1.call-done = bf16[128,2048]{1,0:T(8,128)(2,1)} async-done(((bf16[128,8192]{1,0:T(8,128)(2,1)}), bf16[128,2048]{1,0:T(8,128)(2,1)}) %reduce-scatter.9.cloned.1.call-update) | async-done | bytes 524304 | tf_op jit(solution)/shard_map/reduce_scatter | solution.py:178
  655.2 6.9 all-to-all-start
  665.3 17.6 %all-gather.21.cloned.1.call-done = bf16[128,8192]{1,0:T(8,128)(2,1)} async-done(((bf16[128,2048]{1,0:T(8,128)(2,1)}), bf16[128,8192]{1,0:T(8,128)(2,1)}) %all-gather.21.cloned.1.call-update) | async-done | bytes 2097168 | tf_op jit(solution)/shard_map/all_gather | solution.py:171
  685.0 10.6 %fusion.41 = bf16[128,1280]{1,0:T(8,128)(2,1)S(1)} fusion(bf16[1,8192,1280]{2,1,0:T(8,128)(2,1)} %all-gather.15.cloned.1.call-done, bf16[128,8192]{1,0:T(8,128)(2,1)} %all-gather.21.cloned.1.call-done, f32[128]{0:T(128)S(1)} %add_rsqrt_fusion, f32[8192]{0:T(1024)S(1)} %bitcast.205), kind=kOutput, calls=%fused_computation.43 | convolution fusion | flops 2688712704 | bytes 23429632 | tf_op jit(solution)/shard_map/dot_general | solution.py:173
  696.5 12.8 %fusion.19 = bf16[128,8192]{1,0:T(8,128)(2,1)} fusion(bf16[128,1024]{0,1:T(8,128)(2,1)S(1)} %bitcast.198, bf16[1,8192,1024]{2,1,0:T(8,128)(2,1)} %all-gather.17.cloned.1.call-done), kind=kOutput, calls=%fused_computation.15 | convolution fusion | flops 2148532224 | bytes 19136512 | tf_op jit(solution)/shard_map/dot_general | solution.py:175
  709.3 16.7 %all-to-all-done = bf16[16,64,2048]{2,1,0:T(8,128)(2,1)} async-done(((bf16[16,64,2048]{2,1,0:T(8,128)(2,1)}), bf16[16,64,2048]{2,1,0:T(8,128)(2,1)}, u32[]{:S(2)}, u32[]{:S(2)}) %all-to-all-start) | async-done | bytes 4194336 | tf_op jit(solution)/shard_map/all_to_all | solution.py:193
  726.0 6.5 copy.122
  732.5 5.0 all-to-all-start.1
  742.8 43.2 %all-to-all-done.1 = bf16[16,64,2048]{2,0,1:T(8,128)(2,1)} async-done(((bf16[16,64,2048]{2,0,1:T(8,128)(2,1)}), bf16[16,64,2048]{2,0,1:T(8,128)(2,1)}, u32[]{:S(2)}, u32[]{:S(2)}) %all-to-all-start.1) | async-done | bytes 4194336 | tf_op jit(solution)/shard_map/all_to_all | solution.py:192
  (137 shorter events, 70.5 us)
Async XLA Ops:
  7.2 113.7 %all-gather.9.cloned.1.call-start = ((), (), s32[]{:S(2)}) async-start(), calls=%async_computation.6 | async-start | bytes 10649600 | tf_op jit(solution)/shard_map/all_gather | solution.py:117
  32.9 183.3 %reduce-scatter.5.cloned.1.call-start = ((), (), s32[]{:S(2)}) async-start(), calls=%async_computation.7 | async-start | bytes 8912896 | tf_op jit(solution)/shard_map/reduce_scatter | solution.py:136
  131.6 84.6 %copy-start.9 = (bf16[128,2048]{1,0:T(8,128)(2,1)S(1)}, bf16[128,2048]{1,0:T(8,128)(2,1)}, u32[]{:S(2)}) copy-start(bf16[128,2048]{1,0:T(8,128)(2,1)} %param.22) | copy-start | bytes 1572868
  131.7 101.1 %copy-start.11 = (s32[1,3]{1,0:T(1,128)S(1)}, s32[1,3]{1,0:T(1,128)}, u32[]{:S(2)}) copy-start(s32[1,3]{1,0:T(1,128)} %param.23) | copy-start | bytes 40
  131.7 267.0 %copy-start.12 = (f32[1,8192]{1,0:T(1,128)S(1)}, f32[1,8192]{1,0:T(1,128)}, u32[]{:S(2)}) copy-start(f32[1,8192]{1,0:T(1,128)} %param.24) | copy-start | bytes 98308
  131.7 98.0 %all-gather.11.cloned.1.call-start = ((), (), s32[]{:S(2)}) async-start(), calls=%async_computation.8 | async-start | bytes 1572864 | tf_op jit(solution)/shard_map/all_gather | solution.py:157
  218.2 46.0 %all-gather.13.cloned.1.call-start = ((), (), s32[]{:S(2)}) async-start(), calls=%async_computation.9 | async-start | bytes 2621440 | tf_op jit(solution)/shard_map/all_gather | solution.py:171
  231.6 167.1 %all-gather.15.cloned.1.call-start = ((), (), s32[]{:S(2)}) async-start(), calls=%async_computation.10 | async-start | bytes 22282240 | tf_op jit(solution)/shard_map/all_gather | solution.py:146
  232.2 279.5 %all-gather.17.cloned.1.call-start = ((), (), s32[]{:S(2)}) async-start(), calls=%async_computation.11 | async-start | bytes 17825792 | tf_op jit(solution)/shard_map/all_gather | solution.py:147
  232.7 321.6 %reduce-scatter.7.cloned.1.call-start = ((), (), s32[]{:S(2)}) async-start(), calls=%async_computation.12 | async-start | bytes 2621440 | tf_op jit(solution)/shard_map/reduce_scatter | solution.py:178
  511.7 42.6 %copy-start.4 = (bf16[256,2048]{1,0:T(8,128)(2,1)S(1)}, bf16[256,2048]{1,0:T(8,128)(2,1)}, u32[]{:S(2)}) copy-start(bf16[256,2048]{1,0:T(8,128)(2,1)} %all-gather.11.cloned.1.call-done) | copy-start | bytes 3145732
  524.5 66.0 %all-gather.19.cloned.1.call-start = ((), (), s32[]{:S(2)}) async-start(), calls=%async_computation.13 | async-start | bytes 2621440 | tf_op jit(solution)/shard_map/all_gather | solution.py:171
  555.5 3.3 collective-permute-start
  559.7 87.1 %reduce-scatter.9.cloned.1.call-start = ((), (), s32[]{:S(2)}) async-start(), calls=%async_computation.14 | async-start | bytes 2621440 | tf_op jit(solution)/shard_map/reduce_scatter | solution.py:178
  559.8 3.1 collective-permute-start.1
  604.0 42.7 %copy-start.2 = (bf16[128,2048]{1,0:T(8,128)(2,1)S(1)}, bf16[128,2048]{1,0:T(8,128)(2,1)}, u32[]{:S(2)}) copy-start(bf16[128,2048]{1,0:T(8,128)(2,1)} %slice_select_fusion.1) | copy-start | bytes 1572868
  616.9 66.1 %all-gather.21.cloned.1.call-start = ((), (), s32[]{:S(2)}) async-start(), calls=%async_computation.15 | async-start | bytes 2621440 | tf_op jit(solution)/shard_map/all_gather | solution.py:171
  648.0 3.3 collective-permute-start.2
  655.2 70.8 %all-to-all-start = ((bf16[16,64,2048]{2,1,0:T(8,128)(2,1)}), bf16[16,64,2048]{2,1,0:T(8,128)(2,1)}, u32[]{:S(2)}, u32[]{:S(2)}) async-start(bf16[16,64,2048]{2,1,0:T(8,128)(2,1)} %bitcast.188), calls=%async_computation.4 | async-start | bytes 8388608 | tf_op jit(solution)/shard_map/all_to_all | solution.py:193
  662.1 77.1 %reduce-scatter.11.cloned.1.call-start = ((), (), s32[]{:S(2)}) async-start(), calls=%async_computation.16 | async-start | bytes 2621440 | tf_op jit(solution)/shard_map/reduce_scatter | solution.py:178
  662.1 2.8 collective-permute-start.3
  732.5 53.5 %all-to-all-start.1 = ((bf16[16,64,2048]{2,0,1:T(8,128)(2,1)}), bf16[16,64,2048]{2,0,1:T(8,128)(2,1)}, u32[]{:S(2)}, u32[]{:S(2)}) async-start(bf16[16,64,2048]{2,0,1:T(8,128)(2,1)} %copy.122), calls=%async_computation.5 | async-start | bytes 8388608 | tf_op jit(solution)/shard_map/all_to_all | solution.py:192
  737.5 53.2 %all-reduce.3.cloned.1.call-start = ((), (), s32[]{:S(2)}) async-start(), calls=%async_computation.17 | async-start | bytes 2097152 | tf_op jit(solution)/shard_map/psum | solution.py:25
  740.4 52.1 %copy-start.1 = (bf16[1280,1280]{1,0:T(8,128)(2,1)S(1)}, bf16[1280,1280]{1,0:T(8,128)(2,1)}, u32[]{:S(2)}) copy-start(bf16[1280,1280]{1,0:T(8,128)(2,1)} %param.18) | copy-start | bytes 9830404
  (11 other events, 127.5 us)
Sparse Core Ops, SparseCore 0:
  33.0 87.8 all-gather.8
  131.8 84.4 reduce-scatter.4
  218.5 11.1 all-gather.10
  231.8 32.4 all-gather.12
  266.2 132.4 all-gather.14
  400.7 110.9 all-gather.16
  524.7 29.5 reduce-scatter.6
  559.8 30.6 all-gather.18
  617.0 29.7 reduce-scatter.8
  652.2 30.6 all-gather.20
  709.4 29.7 reduce-scatter.10
  742.9 26.6 all-reduce.2
where the time goes:
time: 808 us; the launch traced here: 800 us
  waiting for transfers between devices  590 us (73%)
  matrix products  97.5 us (12%)
  blocking collectives  27.2 us (3%)
  other arithmetic  27.1 us (3%)
  local copies, waits for them, and re-layouts  21.7 us (3%)
  starting transfers between devices  20.7 us (3%)
  between operations  15.5 us (2%)
    all_gather x1, waiting for transfers between devices, shards(): lax.all_gather(w_qkv, 'dp', axis=1, tiled=True)  132 us
    all_gather x1, waiting for transfers between devices, shards(): lax.all_gather(wo_t, 'dp', axis=1, tiled=True)  102 us
    reduce_scatter x1, waiting for transfers between devices, shards(): lax.psum_scatter(jnp.dot(picked, w_merge, preferred_element_type=jnp.floa...  83.8 us
    all_gather x3, waiting for transfers between devices, shards(): features = lax.all_gather(carried, 'mp', axis=1, tiled=True)  73.8 us
    reduce_scatter x3, waiting for transfers between devices, shards(): lax.psum_scatter(partial_value.astype(jnp.bfloat16), 'mp', scatter_dimens...  61.3 us
    all_gather x1, waiting for transfers between devices, shards(): lax.all_gather(merged, ('dp', 'mp'), axis=0, tiled=True)  60.5 us
    all_to_all x1, waiting for transfers between devices, shards(): lax.all_to_all(lax.all_to_all(outgoing, 'dp', split_axis=0, concat_axis=0...  43.2 us
    dot_general x3, matrix products, shards(): lax.dot_general(attended, out_weight, (((1,), (1,)), ((), ())), preferred...  38.4 us
  transfers between devices with their start and end apart: 18, of which 17 were waited for; matrix products, arithmetic and copies ran while one was open for 8% of the time, Pallas kernels for 0%

commit v1 on v0

--- a/solution.py
+++ b/solution.py
@@ -189,13 +189,10 @@
     )
     outgoing = jnp.dot(picker, row_grads, preferred_element_type=jnp.float32).astype(jnp.bfloat16)
     outgoing = outgoing.reshape(dp_count, section_rows // dp_count, columns)
-    returned = lax.all_to_all(
-        lax.all_to_all(outgoing, "dp", split_axis=0, concat_axis=0, tiled=True),
-        "mp",
-        split_axis=1,
-        concat_axis=2,
-        tiled=True,
-    )
+    x = lax.all_to_all(outgoing, "dp", split_axis=0, concat_axis=0, tiled=True)
+    pieces = jnp.split(x, lax.axis_size("mp"), axis=1)
+    received = lax.all_to_all(jnp.stack(pieces), "mp", 0, 0)
+    returned = jnp.concatenate(received, axis=2)
     merged_grads = jnp.sum(returned.astype(jnp.float32), axis=0).astype(jnp.bfloat16)
     return (final_hidden, merged_grads)
 

time: 808 us -> 806 us (level)
  transfers between devices with their start and end apart: 18 -> 18, of which waited for: 17 -> 17; matrix products, arithmetic and copies ran while one was open for 8% -> 7% of each run, Pallas kernels for 0% -> 0%
where the time goes in v1:
time: 806 us; the launch traced here: 797 us
  waiting for transfers between devices  590 us (73%)
  matrix products  97.5 us (12%)
  other arithmetic  28.4 us (4%)
  blocking collectives  27.2 us (3%)
  starting transfers between devices  20.7 us (3%)
  local copies, waits for them, and re-layouts  18 us (2%)
  between operations  15.5 us (2%)
    all_gather x1, waiting for transfers between devices, shards(): lax.all_gather(w_qkv, 'dp', axis=1, tiled=True)  132 us
    all_gather x1, waiting for transfers between devices, shards(): lax.all_gather(wo_t, 'dp', axis=1, tiled=True)  102 us
    reduce_scatter x1, waiting for transfers between devices, shards(): lax.psum_scatter(jnp.dot(picked, w_merge, preferred_element_type=jnp.floa...  83.8 us
    all_gather x3, waiting for transfers between devices, shards(): features = lax.all_gather(carried, 'mp', axis=1, tiled=True)  73.8 us
    reduce_scatter x3, waiting for transfers between devices, shards(): lax.psum_scatter(partial_value.astype(jnp.bfloat16), 'mp', scatter_dimens...  62.6 us
    all_gather x1, waiting for transfers between devices, shards(): lax.all_gather(merged, ('dp', 'mp'), axis=0, tiled=True)  60.5 us
    all_to_all x1, waiting for transfers between devices, shards(): received = lax.all_to_all(jnp.stack(pieces), 'mp', 0, 0)  41.8 us
    dot_general x3, matrix products, shards(): lax.dot_general(attended, out_weight, (((1,), (1,)), ((), ())), preferred...  38.4 us
  transfers between devices with their start and end apart: 18, of which 17 were waited for; matrix products, arithmetic and copies ran while one was open for 7% of the time, Pallas kernels for 0%

profile of v1, /device:TPU:0, one launch (start us, length us, event | category | flops | bytes accessed | tf_op | source)
XLA Modules:
  0.0 797.3 jit_solution(16667692174789153264)
XLA Ops:
  9.6 6.6 convolution_convert_fusion.1
  34.4 24.9 %all-reduce = s32[1024]{0:T(1024)S(1)} all-reduce(s32[1024]{0:T(1024)S(1)} %bitcast_dynamic-update-slice_fusion), channel_id=1, replica_groups=mesh['section'=2,'dp'=16,'mp'=4] {'dp','mp'}, use_global_device_ids=true, to_apply=%add | all-reduce | flops 1024 | bytes 8192 | tf_op jit(solution)/shard_map/squeeze | solution.py:120
  60.4 60.5 %all-gather.9.cloned.1.call-done = bf16[1024,5120]{1,0:T(8,128)(2,1)} async-done(((bf16[16,5120]{1,0:T(8,128)(2,1)}), bf16[1024,5120]{1,0:T(8,128)(2,1)}) %all-gather.9.cloned.1.call-update) | async-done | bytes 10485776 | tf_op jit(solution)/shard_map/all_gather | solution.py:117
  120.9 10.7 %convolution_convert_fusion = bf16[2048,2048]{1,0:T(8,128)(2,1)} fusion(bf16[320,2048]{1,0:T(8,128)(2,1)} %param.20, s32[1024]{0:T(1024)S(1)} %get-tuple-element.11, bf16[1024,5120]{1,0:T(8,128)(2,1)} %all-gather.9.cloned.1.call-done, s32[]{:T(128)S(6)} %select_n.69), kind=kOutput, calls=%fused_computation.18 | convolution fusion | flops 4033478656 | bytes 10489860 | tf_op jit(solution)/shard_map/dot_general | solution.py:137
  132.4 83.8 %reduce-scatter.5.cloned.1.call-done = bf16[128,2048]{1,0:T(8,128)(2,1)} async-done(((bf16[2048,2048]{1,0:T(8,128)(2,1)}), bf16[128,2048]{1,0:T(8,128)(2,1)}) %reduce-scatter.5.cloned.1.call-update) | async-done | bytes 524304 | tf_op jit(solution)/shard_map/reduce_scatter | solution.py:136
  218.3 11.4 %all-gather.11.cloned.1.call-done = bf16[256,2048]{1,0:T(8,128)(2,1)} async-done(((bf16[128,2048]{1,0:T(8,128)(2,1)}), bf16[256,2048]{1,0:T(8,128)(2,1)}) %all-gather.11.cloned.1.call-update) | async-done | bytes 1048592 | tf_op jit(solution)/shard_map/all_gather | solution.py:157
  235.4 28.8 %all-gather.13.cloned.1.call-done = bf16[128,8192]{1,0:T(8,128)(2,1)} async-done(((bf16[128,2048]{1,0:T(8,128)(2,1)}), bf16[128,8192]{1,0:T(8,128)(2,1)}) %all-gather.13.cloned.1.call-update) | async-done | bytes 2097168 | tf_op jit(solution)/shard_map/all_gather | solution.py:171
  266.3 132.4 %all-gather.15.cloned.1.call-done = bf16[1,8192,1280]{2,1,0:T(8,128)(2,1)} async-done(((bf16[1,512,1280]{2,1,0:T(8,128)(2,1)}), bf16[1,8192,1280]{2,1,0:T(8,128)(2,1)}) %all-gather.15.cloned.1.call-update) | async-done | bytes 20971536 | tf_op jit(solution)/shard_map/all_gather | solution.py:146
  398.7 10.6 %fusion.35 = bf16[128,1280]{1,0:T(8,128)(2,1)S(1)} fusion(bf16[1,8192,1280]{2,1,0:T(8,128)(2,1)} %all-gather.15.cloned.1.call-done, bf16[128,8192]{1,0:T(8,128)(2,1)} %all-gather.13.cloned.1.call-done, f32[8192]{0:T(1024)S(1)} %bitcast.209, f32[128]{0:T(128)S(1)} %add_rsqrt_fusion.2), kind=kOutput, calls=%fused_computation.42 | convolution fusion | flops 2688712704 | bytes 23429632 | tf_op jit(solution)/shard_map/dot_general | solution.py:173
  410.1 101.6 %all-gather.17.cloned.1.call-done = bf16[1,8192,1024]{2,1,0:T(8,128)(2,1)} async-done(((bf16[1,512,1024]{2,1,0:T(8,128)(2,1)}), bf16[1,8192,1024]{2,1,0:T(8,128)(2,1)}) %all-gather.17.cloned.1.call-update) | async-done | bytes 16777232 | tf_op jit(solution)/shard_map/all_gather | solution.py:147
  511.7 12.8 %fusion.13 = bf16[128,8192]{1,0:T(8,128)(2,1)} fusion(bf16[128,1024]{0,1:T(8,128)(2,1)S(1)} %bitcast.203, bf16[1,8192,1024]{2,1,0:T(8,128)(2,1)} %all-gather.17.cloned.1.call-done), kind=kOutput, calls=%fused_computation.13 | convolution fusion | flops 2148532224 | bytes 19136512 | tf_op jit(solution)/shard_map/dot_general | solution.py:175
  524.6 29.7 %reduce-scatter.7.cloned.1.call-done = bf16[128,2048]{1,0:T(8,128)(2,1)} async-done(((bf16[128,8192]{1,0:T(8,128)(2,1)}), bf16[128,2048]{1,0:T(8,128)(2,1)}) %reduce-scatter.7.cloned.1.call-update) | async-done | bytes 524304 | tf_op jit(solution)/shard_map/reduce_scatter | solution.py:178
  563.2 27.3 %all-gather.19.cloned.1.call-done = bf16[128,8192]{1,0:T(8,128)(2,1)} async-done(((bf16[128,2048]{1,0:T(8,128)(2,1)}), bf16[128,8192]{1,0:T(8,128)(2,1)}) %all-gather.19.cloned.1.call-update) | async-done | bytes 2097168 | tf_op jit(solution)/shard_map/all_gather | solution.py:171
  592.6 10.6 %fusion.38 = bf16[128,1280]{1,0:T(8,128)(2,1)S(1)} fusion(bf16[1,8192,1280]{2,1,0:T(8,128)(2,1)} %all-gather.15.cloned.1.call-done, bf16[128,8192]{1,0:T(8,128)(2,1)} %all-gather.19.cloned.1.call-done, f32[128]{0:T(128)S(1)} %add_rsqrt_fusion.1, f32[8192]{0:T(1024)S(1)} %bitcast.210), kind=kOutput, calls=%fused_computation.43 | convolution fusion | flops 2688712704 | bytes 23429632 | tf_op jit(solution)/shard_map/dot_general | solution.py:173
  604.0 12.8 %fusion.16 = bf16[128,8192]{1,0:T(8,128)(2,1)} fusion(bf16[128,1024]{0,1:T(8,128)(2,1)S(1)} %bitcast.205, bf16[1,8192,1024]{2,1,0:T(8,128)(2,1)} %all-gather.17.cloned.1.call-done), kind=kOutput, calls=%fused_computation.14 | convolution fusion | flops 2148532224 | bytes 19136512 | tf_op jit(solution)/shard_map/dot_general | solution.py:175
  616.9 29.9 %reduce-scatter.9.cloned.1.call-done = bf16[128,2048]{1,0:T(8,128)(2,1)} async-done(((bf16[128,8192]{1,0:T(8,128)(2,1)}), bf16[128,2048]{1,0:T(8,128)(2,1)}) %reduce-scatter.9.cloned.1.call-update) | async-done | bytes 524304 | tf_op jit(solution)/shard_map/reduce_scatter | solution.py:178
  652.1 3.1 convolution_convert_fusion.2
  655.2 6.9 all-to-all-start
  665.3 17.6 %all-gather.21.cloned.1.call-done = bf16[128,8192]{1,0:T(8,128)(2,1)} async-done(((bf16[128,2048]{1,0:T(8,128)(2,1)}), bf16[128,8192]{1,0:T(8,128)(2,1)}) %all-gather.21.cloned.1.call-update) | async-done | bytes 2097168 | tf_op jit(solution)/shard_map/all_gather | solution.py:171
  685.0 10.6 %fusion.41 = bf16[128,1280]{1,0:T(8,128)(2,1)S(1)} fusion(bf16[1,8192,1280]{2,1,0:T(8,128)(2,1)} %all-gather.15.cloned.1.call-done, bf16[128,8192]{1,0:T(8,128)(2,1)} %all-gather.21.cloned.1.call-done, f32[128]{0:T(128)S(1)} %add_rsqrt_fusion, f32[8192]{0:T(1024)S(1)} %bitcast.211), kind=kOutput, calls=%fused_computation.44 | convolution fusion | flops 2688712704 | bytes 23429632 | tf_op jit(solution)/shard_map/dot_general | solution.py:173
  696.5 12.8 %fusion.19 = bf16[128,8192]{1,0:T(8,128)(2,1)} fusion(bf16[128,1024]{0,1:T(8,128)(2,1)S(1)} %bitcast.204, bf16[1,8192,1024]{2,1,0:T(8,128)(2,1)} %all-gather.17.cloned.1.call-done), kind=kOutput, calls=%fused_computation.15 | convolution fusion | flops 2148532224 | bytes 19136512 | tf_op jit(solution)/shard_map/dot_general | solution.py:175
  709.3 16.7 %all-to-all-done = bf16[16,64,2048]{2,1,0:T(8,128)(2,1)} async-done(((bf16[16,64,2048]{2,1,0:T(8,128)(2,1)}), bf16[16,64,2048]{2,1,0:T(8,128)(2,1)}, u32[]{:S(2)}, u32[]{:S(2)}) %all-to-all-start) | async-done | bytes 4194336 | tf_op jit(solution)/shard_map/all_to_all | solution.py:192
  731.1 5.0 all-to-all-start.1
  742.8 41.8 %all-to-all-done.1 = bf16[4,16,16,2048]{3,2,1,0:T(8,128)(2,1)} async-done(((bf16[4,16,16,2048]{3,2,1,0:T(8,128)(2,1)}), bf16[4,16,16,2048]{3,2,1,0:T(8,128)(2,1)}, u32[]{:S(2)}, u32[]{:S(2)}) %all-to-all-start.1) | async-done | bytes 4194336 | tf_op jit(solution)/shard_map/all_to_all | solution.py:194
  (138 shorter events, 72.8 us)
Async XLA Ops:
  7.2 113.7 %all-gather.9.cloned.1.call-start = ((), (), s32[]{:S(2)}) async-start(), calls=%async_computation.6 | async-start | bytes 10649600 | tf_op jit(solution)/shard_map/all_gather | solution.py:117
  32.9 183.3 %reduce-scatter.5.cloned.1.call-start = ((), (), s32[]{:S(2)}) async-start(), calls=%async_computation.7 | async-start | bytes 8912896 | tf_op jit(solution)/shard_map/reduce_scatter | solution.py:136
  131.6 84.6 %copy-start.9 = (bf16[128,2048]{1,0:T(8,128)(2,1)S(1)}, bf16[128,2048]{1,0:T(8,128)(2,1)}, u32[]{:S(2)}) copy-start(bf16[128,2048]{1,0:T(8,128)(2,1)} %param.22) | copy-start | bytes 1572868
  131.7 101.1 %copy-start.11 = (s32[1,3]{1,0:T(1,128)S(1)}, s32[1,3]{1,0:T(1,128)}, u32[]{:S(2)}) copy-start(s32[1,3]{1,0:T(1,128)} %param.23) | copy-start | bytes 40
  131.7 267.0 %copy-start.12 = (f32[1,8192]{1,0:T(1,128)S(1)}, f32[1,8192]{1,0:T(1,128)}, u32[]{:S(2)}) copy-start(f32[1,8192]{1,0:T(1,128)} %param.24) | copy-start | bytes 98308
  131.7 98.0 %all-gather.11.cloned.1.call-start = ((), (), s32[]{:S(2)}) async-start(), calls=%async_computation.8 | async-start | bytes 1572864 | tf_op jit(solution)/shard_map/all_gather | solution.py:157
  218.2 46.0 %all-gather.13.cloned.1.call-start = ((), (), s32[]{:S(2)}) async-start(), calls=%async_computation.9 | async-start | bytes 2621440 | tf_op jit(solution)/shard_map/all_gather | solution.py:171
  231.6 167.1 %all-gather.15.cloned.1.call-start = ((), (), s32[]{:S(2)}) async-start(), calls=%async_computation.10 | async-start | bytes 22282240 | tf_op jit(solution)/shard_map/all_gather | solution.py:146
  232.2 279.5 %all-gather.17.cloned.1.call-start = ((), (), s32[]{:S(2)}) async-start(), calls=%async_computation.11 | async-start | bytes 17825792 | tf_op jit(solution)/shard_map/all_gather | solution.py:147
  232.7 321.6 %reduce-scatter.7.cloned.1.call-start = ((), (), s32[]{:S(2)}) async-start(), calls=%async_computation.12 | async-start | bytes 2621440 | tf_op jit(solution)/shard_map/reduce_scatter | solution.py:178
  511.7 42.6 %copy-start.4 = (bf16[256,2048]{1,0:T(8,128)(2,1)S(1)}, bf16[256,2048]{1,0:T(8,128)(2,1)}, u32[]{:S(2)}) copy-start(bf16[256,2048]{1,0:T(8,128)(2,1)} %all-gather.11.cloned.1.call-done) | copy-start | bytes 3145732
  524.5 66.0 %all-gather.19.cloned.1.call-start = ((), (), s32[]{:S(2)}) async-start(), calls=%async_computation.13 | async-start | bytes 2621440 | tf_op jit(solution)/shard_map/all_gather | solution.py:171
  555.5 3.3 collective-permute-start
  559.7 87.1 %reduce-scatter.9.cloned.1.call-start = ((), (), s32[]{:S(2)}) async-start(), calls=%async_computation.14 | async-start | bytes 2621440 | tf_op jit(solution)/shard_map/reduce_scatter | solution.py:178
  559.8 3.1 collective-permute-start.1
  604.0 42.7 %copy-start.2 = (bf16[128,2048]{1,0:T(8,128)(2,1)S(1)}, bf16[128,2048]{1,0:T(8,128)(2,1)}, u32[]{:S(2)}) copy-start(bf16[128,2048]{1,0:T(8,128)(2,1)} %slice_select_fusion.1) | copy-start | bytes 1572868
  616.9 66.1 %all-gather.21.cloned.1.call-start = ((), (), s32[]{:S(2)}) async-start(), calls=%async_computation.15 | async-start | bytes 2621440 | tf_op jit(solution)/shard_map/all_gather | solution.py:171
  648.0 3.3 collective-permute-start.2
  655.2 70.8 %all-to-all-start = ((bf16[16,64,2048]{2,1,0:T(8,128)(2,1)}), bf16[16,64,2048]{2,1,0:T(8,128)(2,1)}, u32[]{:S(2)}, u32[]{:S(2)}) async-start(bf16[16,64,2048]{2,1,0:T(8,128)(2,1)} %bitcast.194), calls=%async_computation.4 | async-start | bytes 8388608 | tf_op jit(solution)/shard_map/all_to_all | solution.py:192
  662.1 77.1 %reduce-scatter.11.cloned.1.call-start = ((), (), s32[]{:S(2)}) async-start(), calls=%async_computation.16 | async-start | bytes 2621440 | tf_op jit(solution)/shard_map/reduce_scatter | solution.py:178
  662.1 2.8 collective-permute-start.3
  731.1 53.5 %all-to-all-start.1 = ((bf16[4,16,16,2048]{3,2,1,0:T(8,128)(2,1)}), bf16[4,16,16,2048]{3,2,1,0:T(8,128)(2,1)}, u32[]{:S(2)}, u32[]{:S(2)}) async-start(bf16[4,16,16,2048]{3,2,1,0:T(8,128)(2,1)} %pad_maximum_fusion), calls=%async_computation.5 | async-start | bytes 8388608 | tf_op jit(solution)/shard_map/all_to_all | solution.py:194
  736.1 52.2 %all-reduce.3.cloned.1.call-start = ((), (), s32[]{:S(2)}) async-start(), calls=%async_computation.17 | async-start | bytes 2097152 | tf_op jit(solution)/shard_map/psum | solution.py:25
  740.4 49.8 %copy-start.1 = (bf16[1280,1280]{1,0:T(8,128)(2,1)S(1)}, bf16[1280,1280]{1,0:T(8,128)(2,1)}, u32[]{:S(2)}) copy-start(bf16[1280,1280]{1,0:T(8,128)(2,1)} %param.18) | copy-start | bytes 9830404
  (11 other events, 128.9 us)
Sparse Core Ops, SparseCore 0:
  33.0 87.8 all-gather.8
  131.8 84.4 reduce-scatter.4
  218.5 11.1 all-gather.10
  231.8 32.4 all-gather.12
  266.2 132.4 all-gather.14
  400.7 110.9 all-gather.16
  524.7 29.5 reduce-scatter.6
  559.8 30.6 all-gather.18
  617.0 29.7 reduce-scatter.8
  652.2 30.6 all-gather.20
  709.4 29.7 reduce-scatter.10
  742.9 28.0 all-reduce.2
